TPU v7x, 32 devices: a whole 2x2x4 slice. The times are simulated.
32 devices in a mesh: blk: 8 (over z, x), sub: 4 (over y, core).
Axes of the slice: x: 2, y: 2, z: 4, core: 2. Of those that a mesh axis runs over, the one named last changes fastest.
Arguments:
- features: bfloat16 [12288, 768], P(('blk', 'sub')), may hold values from -6 to 6
- scales: bfloat16 [12288], P('blk'), may hold values from 0.5 to 4
- neighbor_lists: int32 [9, 16, 12288], P(None, None, 'blk'), may hold values from 0 to 1535, as said below
- eigen_block: float32 [64, 12288], P(None, ('blk', 'sub')), may hold values from -6 to 6
Outputs:
- embedding: float32 [64, 12288], P(None, ('blk', 'sub'))
Inputs may be any that keep to these rules, and one draw needn't show every extreme that they name: For each j and point p, the 16 entries neighbor_lists[j, :, p] are distinct positions within the row block that lies j - 4 blocks before p's block, counted cyclically.
All inputs are finite; a program needn't handle non-finite values.
Results may differ from a plain program's by a relative error of at most 0.0039.
Values may be sent and summed in bfloat16 or wider, within the bound.
A program may use at most 128 MiB of HBM per device.

v0:
```python
import math
import jax
import jax.numpy as jnp
from jax import lax
from jax.sharding import PartitionSpec as P

F = 768


def as_sent(value):
    return jax.tree.map(lambda a: a.astype(jnp.bfloat16) if a.dtype == jnp.float32 else a, value)


def shifted(value, axis, steps):
    count = lax.axis_size(axis)
    pairs = [(source, (source + steps) % count) for source in range(count)]
    return lax.ppermute(value, axis, pairs)


def pair_weights(
    block_feats, block_norms, block_scales, lists_here, positions, moving_feats, moving_scales
):
    inner = lax.dot_general(
        block_feats, moving_feats, (((1,), (1,)), ((), ())), preferred_element_type=jnp.float32
    )
    moving_norms = jnp.sum(jnp.square(moving_feats.astype(jnp.float32)), axis=1)
    distance = block_norms[:, None] + moving_norms[None, :] - 2.0 * inner
    spread = F * block_scales[:, None] * moving_scales.astype(jnp.float32)[None, :]
    affinity = jnp.exp(-distance / spread)
    listed = jnp.sum(
        (lists_here[:, :, None] == positions[None, None, :]).astype(jnp.float32), axis=0
    )
    return affinity * listed


def band_sweep(payload, work, half):
    row_total, col_total = work(half, payload)
    for heading in (1, -1):
        pieces = payload
        owed = []
        for travel in range(1, half + 1):
            pieces = jax.tree.map(
                lambda part, own: part.astype(own.dtype),
                shifted(as_sent(pieces), "blk", heading),
                pieces,
            )
            row_term, col_term = work(heading * travel + half, pieces)
            row_total = row_total + row_term
            owed.append(col_term)
        carried = jnp.zeros_like(owed[0])
        for travel in range(half - 1, -1, -1):
            carried = shifted(carried + owed[travel], "blk", -heading)
        col_total = col_total + carried
    return (row_total, col_total)


def to_owners(terms):
    return lax.psum_scatter(terms, "sub", scatter_dimension=1, tiled=True)


def local(features, scales, neighbor_lists, eigen_block):
    rows_dev = features.shape[0]
    sub_index = lax.axis_index("sub")
    half = (neighbor_lists.shape[0] - 1) // 2
    block_feats = lax.all_gather(features, "sub", axis=0, tiled=True)
    block_norms = jnp.sum(jnp.square(block_feats.astype(jnp.float32)), axis=1)
    block_scales = scales.astype(jnp.float32)
    own_scales = lax.dynamic_slice_in_dim(scales, sub_index * rows_dev, rows_dev)
    positions = sub_index * rows_dev + jnp.arange(rows_dev, dtype=jnp.int32)

    def weights(shift_index, pieces):
        return pair_weights(
            block_feats,
            block_norms,
            block_scales,
            neighbor_lists[shift_index],
            positions,
            pieces[0],
            pieces[1],
        )

    def degree_work(shift_index, pieces):
        tile = weights(shift_index, pieces)
        return (jnp.sum(tile, axis=1)[None, :], jnp.sum(tile, axis=0)[None, :])

    row_deg, col_deg = band_sweep((features, own_scales), degree_work, half)
    degree = 1.0 + 0.5 * (to_owners(row_deg) + col_deg)
    inv_root = lax.rsqrt(degree)
    scaled = eigen_block * inv_root
    scaled_low = scaled.astype(jnp.bfloat16)
    block_eigen = lax.all_gather(scaled_low, "sub", axis=1, tiled=True)

    def product_work(shift_index, pieces):
        tile = weights(shift_index, pieces).astype(jnp.bfloat16)
        moving_eigen = pieces[2]
        row_term = lax.dot_general(
            moving_eigen, tile, (((1,), (1,)), ((), ())), preferred_element_type=jnp.float32
        )
        col_term = jnp.dot(block_eigen, tile, preferred_element_type=jnp.float32)
        return (row_term, col_term)

    product_payload = (features, own_scales, scaled_low)
    row_side, col_side = band_sweep(product_payload, product_work, half)
    mixed = inv_root * (scaled + 0.5 * (to_owners(row_side) + col_side))
    partial_gram = jnp.dot(
        mixed, mixed.T, precision=lax.Precision.HIGHEST, preferred_element_type=jnp.float32
    )
    gram = lax.psum(partial_gram, ("blk", "sub"))
    lower = jnp.linalg.cholesky(gram)
    total_rows = rows_dev * lax.axis_size("blk") * lax.axis_size("sub")
    return math.sqrt(total_rows) * jax.scipy.linalg.solve_triangular(lower, mixed, lower=True)


def solution(mesh):
    placed = (P(("blk", "sub"), None), P("blk"), P(None, None, "blk"), P(None, ("blk", "sub")))
    return jax.shard_map(
        local, mesh=mesh, in_specs=placed, out_specs=P(None, ("blk", "sub")), check_vma=False
    )
```

profile of v0, /device:TPU:10, one launch (start us, length us, event | category | flops | bytes accessed | tf_op | source)
XLA Modules:
  0.0 344.4 jit_solution(11951891037983374221)
XLA Ops:
  15.0 20.4 %collective-permute-done.1 = bf16[384]{0:T(512)(128)(2,1)S(1)} collective-permute-done((bf16[384]{0:T(512)(128)(2,1)S(1)}, bf16[384]{0:T(512)(128)(2,1)S(1)}, u32[]{:S(2)}, u32[]{:S(2)}) %collective-permute-start.1) | collective-permute-done | bytes 800 | tf_op jit(solution)/shard_map/ppermute | solution.py:17
  39.4 44.8 %convert_reduce_fusion.7 = (f32[1536,384]{1,0:T(8,128)}, f32[1536,384]{1,0:T(8,128)}, f32[1536,384]{1,0:T(8,128)}, f32[1536,384]{1,0:T(8,128)}, f32[1536,384]{1,...) fusion(s32[16,1536]{1,0:T(8,128)S(1)} %get-tuple-element.40, ...), kind=kLoop, calls=%fused_computation.7 | loop fusion | flops 249495552 | bytes 22119936 | tf_op jit(solution)/shard_map/reduce_sum | solution.py:30
  84.3 2.4 collective-permute-start.5
  86.7 2.9 collective-permute-start.4
  97.1 15.2 %collective-permute-done.7 = bf16[384]{0:T(512)(128)(2,1)S(1)} collective-permute-done((bf16[384]{0:T(512)(128)(2,1)S(1)}, bf16[384]{0:T(512)(128)(2,1)S(1)}, u32[]{:S(2)}, u32[]{:S(2)}) %collective-permute-start.7) | collective-permute-done | bytes 800 | tf_op jit(solution)/shard_map/ppermute | solution.py:17
  119.7 6.8 %collective-permute-done.6 = bf16[384,768]{1,0:T(8,128)(2,1)S(1)} collective-permute-done((bf16[384,768]{1,0:T(8,128)(2,1)S(1)}, bf16[384,768]{1,0:T(8,128)(2,1)S(1)}, u32[]{:S(2)}, u32[]{:S(2)}) %collective-permute-start.6) | collective-permute-done | bytes 589856 | tf_op jit(solution)/shard_map/ppermute | solution.py:17
  127.3 14.6 %collective-permute-done.14 = bf16[384,768]{1,0:T(8,128)(2,1)S(1)} collective-permute-done((bf16[384,768]{1,0:T(8,128)(2,1)S(1)}, bf16[384,768]{1,0:T(8,128)(2,1)S(1)}, u32[]{:S(2)}, u32[]{:S(2)}) %collective-permute-start.14) | collective-permute-done | bytes 589856 | tf_op jit(solution)/shard_map/ppermute | solution.py:17
  143.5 2.3 multiply_reduce_fusion
  145.9 4.2 %fusion.40 = (f32[384]{0:T(512)S(1)}, f32[1536]{0:T(1024)S(1)}, bf16[1536,384]{1,0:T(8,128)(2,1)S(1)}) fusion(f32[1536,384]{1,0:T(8,128)} %get-tuple-element.26, f32[384]{0:T(512)} %convert_element_type.159, f32[1536]{0:T(1024)S(1)} %convert_multiply_fusion, bf16[1536,768]{1,0:T(8,128)(2,1)S(1)} %copy-done.8, bf16[384,768]{1,0:T(8,128)(2,1)} %copy-done.26, ...), kind=kOutput, calls=%fused_computation.114 | convolution fusion | flops 911865984 | bytes 6511104 | tf_op jit(solution)/shard_map/dot_general | solution.py:23
  150.7 2.0 collective-permute-start.16
  152.7 3.4 fusion.44
  157.7 4.0 %fusion.39 = (f32[384]{0:T(512)}, f32[1536]{0:T(1024)S(1)}, bf16[1536,384]{1,0:T(8,128)(2,1)}) fusion(f32[1536,384]{1,0:T(8,128)S(1)} %copy-done.16, f32[384]{0:T(512)S(1)} %copy-done.41, f32[1536]{0:T(1024)S(1)} %convert_multiply_fusion, bf16[1536,768]{1,0:T(8,128)(2,1)S(1)} %copy-done.8, bf16[384,768]{1,0:T(8,128)(2,1)S(1)} %copy-done.23, ...), kind=kOutput, calls=%fused_computation.113 | convolution fusion | flops 911865984 | bytes 6511104 | tf_op jit(solution)/shard_map/dot_general | solution.py:23
  161.7 4.0 %fusion.38 = (f32[384]{0:T(512)}, f32[1536]{0:T(1024)S(1)}, bf16[1536,384]{1,0:T(8,128)(2,1)}) fusion(f32[1536,384]{1,0:T(8,128)S(1)} %copy-done.15, f32[384]{0:T(512)S(1)} %copy-done.40, f32[1536]{0:T(1024)S(1)} %convert_multiply_fusion, bf16[1536,768]{1,0:T(8,128)(2,1)S(1)} %copy-done.8, bf16[384,768]{1,0:T(8,128)(2,1)S(1)} %copy-done.19, ...), kind=kOutput, calls=%fused_computation.112 | convolution fusion | flops 911865984 | bytes 6511104 | tf_op jit(solution)/shard_map/dot_general | solution.py:23
  165.7 3.9 %fusion.37 = (f32[384]{0:T(512)}, f32[1536]{0:T(1024)S(1)}, bf16[1536,384]{1,0:T(8,128)(2,1)}) fusion(f32[1536,384]{1,0:T(8,128)S(1)} %copy-done.14, f32[384]{0:T(512)S(1)} %copy-done.38, f32[1536]{0:T(1024)S(1)} %convert_multiply_fusion, bf16[1536,768]{1,0:T(8,128)(2,1)S(1)} %copy-done.8, bf16[384,768]{1,0:T(8,128)(2,1)S(1)} %collective-permute-done, ...), kind=kOutput, calls=%fused_computation.111 | convolution fusion | flops 911865984 | bytes 6511104 | tf_op jit(solution)/shard_map/dot_general | solution.py:23
  169.7 3.9 %fusion.43 = (f32[384]{0:T(512)}, f32[1536]{0:T(1024)S(1)}, bf16[1536,384]{1,0:T(8,128)(2,1)}) fusion(f32[1536,384]{1,0:T(8,128)S(1)} %copy-done.13, f32[384]{0:T(512)S(1)} %copy-done.39, f32[1536]{0:T(1024)S(1)} %convert_multiply_fusion, bf16[1536,768]{1,0:T(8,128)(2,1)S(1)} %copy-done.8, bf16[384,768]{1,0:T(8,128)(2,1)S(1)} %copy-done.21, ...), kind=kOutput, calls=%fused_computation.117 | convolution fusion | flops 911865984 | bytes 6511104 | tf_op jit(solution)/shard_map/dot_general | solution.py:23
  173.7 4.1 %fusion.42 = (f32[384]{0:T(512)}, f32[1536]{0:T(1024)S(1)}, bf16[1536,384]{1,0:T(8,128)(2,1)}) fusion(f32[1536,384]{1,0:T(8,128)S(1)} %copy-done.12, f32[384]{0:T(512)S(1)} %copy-done.37, f32[1536]{0:T(1024)S(1)} %convert_multiply_fusion, bf16[1536,768]{1,0:T(8,128)(2,1)S(1)} %copy-done.8, bf16[384,768]{1,0:T(8,128)(2,1)S(1)} %collective-permute-done.10, ...), kind=kOutput, calls=%fused_computation.116 | convolution fusion | flops 911865984 | bytes 6511104 | tf_op jit(solution)/shard_map/dot_general | solution.py:23
  177.7 3.4 fusion.41
  181.2 2.6 fusion.36
  185.8 5.4 %collective-permute-start.17 = (f32[1,384]{1,0:T(1,128)S(1)}, f32[1,384]{1,0:T(1,128)S(1)}, u32[]{:S(2)}, u32[]{:S(2)}) collective-permute-start(f32[1,384]{1,0:T(1,128)S(1)} %reshape_add_fusion.5), channel_id=1, source_target_pairs={{0,28},{4,0},{8,4},{12,8},{16,12},{20,16},{24,20},{28,24},{1,29},{... | collective-permute-start | bytes 4616 | tf_op jit(solution)/shard_map/ppermute | solution.py:17
  192.5 2.9 collective-permute-start.18
  197.0 2.9 collective-permute-start.19
  200.9 17.3 %reduce-scatter.7.cloned.1.call-done = f32[384,1]{1,0:T(8,128)} async-done(((f32[1536,1]{1,0:T(8,128)}), f32[384,1]{1,0:T(8,128)}) %reduce-scatter.7.cloned.1.call-update) | async-done | bytes 1552
  219.3 5.7 %all_gather.7 = bf16[64,1536]{1,0:T(8,128)(2,1)S(1)} all-gather(bf16[64,384]{1,0:T(8,128)(2,1)S(1)} %multiply_convert_fusion), channel_id=1, replica_groups=mesh['blk'=8,'sub'=4] {'sub'}, dimensions={1}, use_global_device_ids=true | all-gather | bytes 245760 | tf_op jit(solution)/shard_map/all_gather | solution.py:91
  237.6 2.1 collective-permute-done.25
  257.2 2.6 collective-permute-start.34
  261.6 2.7 collective-permute-done.34
  264.3 2.5 collective-permute-start.35
  269.7 2.2 collective-permute-done.35
  273.0 7.3 %reduce-scatter.5.cloned.1.call-done = f32[64,384]{1,0:T(8,128)} async-done(((f32[64,1536]{1,0:T(8,128)}), f32[64,384]{1,0:T(8,128)}) %reduce-scatter.5.cloned.1.call-update) | async-done | bytes 98320 | tf_op jit(solution)/shard_map/reduce_scatter | solution.py:58
  281.5 43.3 %psum.7 = f32[64,64]{0,1:T(8,128)S(1)} all-reduce(f32[64,64]{0,1:T(8,128)S(1)} %fusion.46), channel_id=1, replica_groups=mesh['blk'=8,'sub'=4] {'blk','sub'}, use_global_device_ids=true, to_apply=%region_39.0 | all-reduce | flops 4096 | bytes 32768 | tf_op jit(solution)/shard_map/psum | solution.py:108
  324.8 5.8 %cholesky.16 = f32[64,64]{1,0:T(8,128)S(1)} custom-call(f32[64,64]{1,0:T(8,128)S(1)} %fusion.35), custom_call_target="Cholesky" | custom-call | tf_op jit(solution)/shard_map/jit(cholesky)/cholesky | solution.py:109
  332.0 4.9 %custom-call.7 = f32[1,64,64]{1,2,0:T(8,128)S(1)} custom-call(f32[1,64,64]{2,1,0:T(8,128)S(1)} %fusion.33), custom_call_target="InvertDiagBlocksLowerTriangular" | custom-call | tf_op jit(solution)/shard_map/jit(_solve_triangular)/triangular_solve | solution.py:111
  (234 shorter events, 77.7 us)
Async XLA Ops:
  6.5 136.9 %all-gather.2.cloned.1.call-start = ((), (), s32[]{:S(2)}) async-start(), calls=%async_computation.2 | async-start | bytes 2949120 | tf_op jit(solution)/shard_map/all_gather | solution.py:65
  7.3 210.9 %reduce-scatter.7.cloned.1.call-start = ((), (), s32[]{:S(2)}) async-start(), calls=%async_computation.4 | async-start | bytes 983040
  7.3 30.1 %collective-permute-start = (bf16[384,768]{1,0:T(8,128)(2,1)}, bf16[384,768]{1,0:T(8,128)(2,1)S(1)}, u32[]{:S(2)}, u32[]{:S(2)}) collective-permute-start(bf16[384,768]{1,0:T(8,128)(2,1)} %param.4), channel_id=1, source_target_pairs={{0,4},{4,8},{8,12},{12,16},{16,20},{20,24},{24,28},{28,0},{1,5},{5... | collective-permute-start | bytes 1769480 | tf_op jit(solution)/shard_map/ppermute | solution.py:17
  10.2 25.1 %collective-permute-start.1 = (bf16[384]{0:T(512)(128)(2,1)S(1)}, bf16[384]{0:T(512)(128)(2,1)S(1)}, u32[]{:S(2)}, u32[]{:S(2)}) collective-permute-start(bf16[384]{0:T(512)(128)(2,1)S(1)} %get-tuple-element.33), channel_id=1, source_target_pairs={{0,4},{4,8},{8,12},{12,16},{16,20},{20,24},{24,28},{28,0},{1,5},{5... | collective-permute-start | bytes 2312 | tf_op jit(solution)/shard_map/ppermute | solution.py:17
  11.7 24.2 %collective-permute-start.9 = (bf16[384]{0:T(512)(128)(2,1)S(1)}, bf16[384]{0:T(512)(128)(2,1)S(1)}, u32[]{:S(2)}, u32[]{:S(2)}) collective-permute-start(bf16[384]{0:T(512)(128)(2,1)S(1)} %get-tuple-element.33), channel_id=1, source_target_pairs={{0,28},{4,0},{8,4},{12,8},{16,12},{20,16},{24,20},{28,24},{1,29},{... | collective-permute-start | bytes 2312 | tf_op jit(solution)/shard_map/ppermute | solution.py:17
  12.3 26.6 %collective-permute-start.8 = (bf16[384,768]{1,0:T(8,128)(2,1)}, bf16[384,768]{1,0:T(8,128)(2,1)S(1)}, u32[]{:S(2)}, u32[]{:S(2)}) collective-permute-start(bf16[384,768]{1,0:T(8,128)(2,1)} %param.4), channel_id=1, source_target_pairs={{0,28},{4,0},{8,4},{12,8},{16,12},{20,16},{24,20},{28,24},{1,29},{... | collective-permute-start | bytes 1769480 | tf_op jit(solution)/shard_map/ppermute | solution.py:17
  35.4 48.9 %collective-permute-start.3 = (bf16[384]{0:T(512)(128)(2,1)S(1)}, bf16[384]{0:T(512)(128)(2,1)S(1)}, u32[]{:S(2)}, u32[]{:S(2)}) collective-permute-start(bf16[384]{0:T(512)(128)(2,1)S(1)} %collective-permute-done.1), channel_id=1, source_target_pairs={{0,4},{4,8},{8,12},{12,16},{16,20},{20,24},{24,28},{28,0},{1,5},{5... | collective-permute-start | bytes 2312 | tf_op jit(solution)/shard_map/ppermute | solution.py:17
  36.0 50.7 %collective-permute-start.11 = (bf16[384]{0:T(512)(128)(2,1)S(1)}, bf16[384]{0:T(512)(128)(2,1)S(1)}, u32[]{:S(2)}, u32[]{:S(2)}) collective-permute-start(bf16[384]{0:T(512)(128)(2,1)S(1)} %collective-permute-done.9), channel_id=1, source_target_pairs={{0,28},{4,0},{8,4},{12,8},{16,12},{20,16},{24,20},{28,24},{1,29},{... | collective-permute-start | bytes 2312 | tf_op jit(solution)/shard_map/ppermute | solution.py:17
  37.4 49.3 %collective-permute-start.2 = (bf16[384,768]{1,0:T(8,128)(2,1)S(1)}, bf16[384,768]{1,0:T(8,128)(2,1)S(1)}, u32[]{:S(2)}, u32[]{:S(2)}) collective-permute-start(bf16[384,768]{1,0:T(8,128)(2,1)S(1)} %collective-permute-done), channel_id=1, source_target_pairs={{0,4},{4,8},{8,12},{12,16},{16,20},{20,24},{24,28},{28,0},{1,5},{5... | collective-permute-start | bytes 1769480 | tf_op jit(solution)/shard_map/ppermute | solution.py:17
  38.9 52.8 %collective-permute-start.10 = (bf16[384,768]{1,0:T(8,128)(2,1)S(1)}, bf16[384,768]{1,0:T(8,128)(2,1)S(1)}, u32[]{:S(2)}, u32[]{:S(2)}) collective-permute-start(bf16[384,768]{1,0:T(8,128)(2,1)S(1)} %collective-permute-done.8), channel_id=1, source_target_pairs={{0,28},{4,0},{8,4},{12,8},{16,12},{20,16},{24,20},{28,24},{1,29},{... | collective-permute-start | bytes 1769480 | tf_op jit(solution)/shard_map/ppermute | solution.py:17
  84.3 5.4 %collective-permute-start.5 = (bf16[384]{0:T(512)(128)(2,1)S(1)}, bf16[384]{0:T(512)(128)(2,1)S(1)}, u32[]{:S(2)}, u32[]{:S(2)}) collective-permute-start(bf16[384]{0:T(512)(128)(2,1)S(1)} %collective-permute-done.3), channel_id=1, source_target_pairs={{0,4},{4,8},{8,12},{12,16},{16,20},{20,24},{24,28},{28,0},{1,5},{5... | collective-permute-start | bytes 2312 | tf_op jit(solution)/shard_map/ppermute | solution.py:17
  86.7 27.8 %collective-permute-start.4 = (bf16[384,768]{1,0:T(8,128)(2,1)S(1)}, bf16[384,768]{1,0:T(8,128)(2,1)S(1)}, u32[]{:S(2)}, u32[]{:S(2)}) collective-permute-start(bf16[384,768]{1,0:T(8,128)(2,1)S(1)} %collective-permute-done.2), channel_id=1, source_target_pairs={{0,4},{4,8},{8,12},{12,16},{16,20},{20,24},{24,28},{28,0},{1,5},{5... | collective-permute-start | bytes 1769480 | tf_op jit(solution)/shard_map/ppermute | solution.py:17
  89.6 22.7 %collective-permute-start.7 = (bf16[384]{0:T(512)(128)(2,1)S(1)}, bf16[384]{0:T(512)(128)(2,1)S(1)}, u32[]{:S(2)}, u32[]{:S(2)}) collective-permute-start(bf16[384]{0:T(512)(128)(2,1)S(1)} %collective-permute-done.5), channel_id=1, source_target_pairs={{0,4},{4,8},{8,12},{12,16},{16,20},{20,24},{24,28},{28,0},{1,5},{5... | collective-permute-start | bytes 2312 | tf_op jit(solution)/shard_map/ppermute | solution.py:17
  91.2 21.7 %collective-permute-start.15 = (bf16[384]{0:T(512)(128)(2,1)S(1)}, bf16[384]{0:T(512)(128)(2,1)S(1)}, u32[]{:S(2)}, u32[]{:S(2)}) collective-permute-start(bf16[384]{0:T(512)(128)(2,1)S(1)} %collective-permute-done.13), channel_id=1, source_target_pairs={{0,28},{4,0},{8,4},{12,8},{16,12},{20,16},{24,20},{28,24},{1,29},{... | collective-permute-start | bytes 2312 | tf_op jit(solution)/shard_map/ppermute | solution.py:17
  91.7 24.2 %collective-permute-start.12 = (bf16[384,768]{1,0:T(8,128)(2,1)S(1)}, bf16[384,768]{1,0:T(8,128)(2,1)S(1)}, u32[]{:S(2)}, u32[]{:S(2)}) collective-permute-start(bf16[384,768]{1,0:T(8,128)(2,1)S(1)} %collective-permute-done.10), channel_id=1, source_target_pairs={{0,28},{4,0},{8,4},{12,8},{16,12},{20,16},{24,20},{28,24},{1,29},{... | collective-permute-start | bytes 1769480 | tf_op jit(solution)/shard_map/ppermute | solution.py:17
  114.5 12.0 %collective-permute-start.6 = (bf16[384,768]{1,0:T(8,128)(2,1)S(1)}, bf16[384,768]{1,0:T(8,128)(2,1)S(1)}, u32[]{:S(2)}, u32[]{:S(2)}) collective-permute-start(bf16[384,768]{1,0:T(8,128)(2,1)S(1)} %collective-permute-done.4), channel_id=1, source_target_pairs={{0,4},{4,8},{8,12},{12,16},{16,20},{20,24},{24,28},{28,0},{1,5},{5... | collective-permute-start | bytes 1769480 | tf_op jit(solution)/shard_map/ppermute | solution.py:17
  115.9 26.0 %collective-permute-start.14 = (bf16[384,768]{1,0:T(8,128)(2,1)S(1)}, bf16[384,768]{1,0:T(8,128)(2,1)S(1)}, u32[]{:S(2)}, u32[]{:S(2)}) collective-permute-start(bf16[384,768]{1,0:T(8,128)(2,1)S(1)} %collective-permute-done.12), channel_id=1, source_target_pairs={{0,28},{4,0},{8,4},{12,8},{16,12},{20,16},{24,20},{28,24},{1,29},{... | collective-permute-start | bytes 1769480 | tf_op jit(solution)/shard_map/ppermute | solution.py:17
  150.7 34.4 %collective-permute-start.16 = (f32[1,384]{1,0:T(1,128)}, f32[1,384]{1,0:T(1,128)}, u32[]{:S(2)}, u32[]{:S(2)}) collective-permute-start(f32[1,384]{1,0:T(1,128)} %broadcast_in_dim.20), channel_id=1, source_target_pairs={{0,28},{4,0},{8,4},{12,8},{16,12},{20,16},{24,20},{28,24},{1,29},{... | collective-permute-start | bytes 4616 | tf_op jit(solution)/shard_map/ppermute | solution.py:17
  156.7 34.5 %collective-permute-start.20 = (f32[1,384]{1,0:T(1,128)}, f32[1,384]{1,0:T(1,128)}, u32[]{:S(2)}, u32[]{:S(2)}) collective-permute-start(f32[1,384]{1,0:T(1,128)} %broadcast_in_dim.24), channel_id=1, source_target_pairs={{0,4},{4,8},{8,12},{12,16},{16,20},{20,24},{24,28},{28,0},{1,5},{5... | collective-permute-start | bytes 4616 | tf_op jit(solution)/shard_map/ppermute | solution.py:17
  185.1 95.2 %reduce-scatter.5.cloned.1.call-start = ((), (), s32[]{:S(2)}) async-start(), calls=%async_computation.3 | async-start | bytes 491520 | tf_op jit(solution)/shard_map/reduce_scatter | solution.py:58
  185.8 6.7 %collective-permute-start.17 = (f32[1,384]{1,0:T(1,128)S(1)}, f32[1,384]{1,0:T(1,128)S(1)}, u32[]{:S(2)}, u32[]{:S(2)}) collective-permute-start(f32[1,384]{1,0:T(1,128)S(1)} %reshape_add_fusion.5), channel_id=1, source_target_pairs={{0,28},{4,0},{8,4},{12,8},{16,12},{20,16},{24,20},{28,24},{1,29},{... | collective-permute-start | bytes 4616 | tf_op jit(solution)/shard_map/ppermute | solution.py:17
  197.0 22.2 %collective-permute-start.19 = (f32[1,384]{1,0:T(1,128)S(1)}, f32[1,384]{1,0:T(1,128)S(1)}, u32[]{:S(2)}, u32[]{:S(2)}) collective-permute-start(f32[1,384]{1,0:T(1,128)S(1)} %reshape_add_fusion.3), channel_id=1, source_target_pairs={{0,28},{4,0},{8,4},{12,8},{16,12},{20,16},{24,20},{28,24},{1,29},{... | collective-permute-start | bytes 4616 | tf_op jit(solution)/shard_map/ppermute | solution.py:17
  200.9 18.4 %collective-permute-start.23 = (f32[1,384]{1,0:T(1,128)S(1)}, f32[1,384]{1,0:T(1,128)S(1)}, u32[]{:S(2)}, u32[]{:S(2)}) collective-permute-start(f32[1,384]{1,0:T(1,128)S(1)} %reshape_add_fusion), channel_id=1, source_target_pairs={{0,4},{4,8},{8,12},{12,16},{16,20},{20,24},{24,28},{28,0},{1,5},{5... | collective-permute-start | bytes 4616 | tf_op jit(solution)/shard_map/ppermute | solution.py:17
  225.0 9.4 %collective-permute-start.24 = (bf16[64,384]{1,0:T(8,128)(2,1)S(1)}, bf16[64,384]{1,0:T(8,128)(2,1)S(1)}, u32[]{:S(2)}, u32[]{:S(2)}) collective-permute-start(bf16[64,384]{1,0:T(8,128)(2,1)S(1)} %multiply_convert_fusion), channel_id=1, source_target_pairs={{0,4},{4,8},{8,12},{12,16},{16,20},{20,24},{24,28},{28,0},{1,5},{5... | collective-permute-start | bytes 147464 | tf_op jit(solution)/shard_map/ppermute | solution.py:17
  226.5 10.0 %collective-permute-start.28 = (bf16[64,384]{1,0:T(8,128)(2,1)S(1)}, bf16[64,384]{1,0:T(8,128)(2,1)S(1)}, u32[]{:S(2)}, u32[]{:S(2)}) collective-permute-start(bf16[64,384]{1,0:T(8,128)(2,1)S(1)} %multiply_convert_fusion), channel_id=1, source_target_pairs={{0,28},{4,0},{8,4},{12,8},{16,12},{20,16},{24,20},{28,24},{1,29},{... | collective-permute-start | bytes 147464 | tf_op jit(solution)/shard_map/ppermute | solution.py:17
  230.6 11.7 %collective-permute-start.32 = (f32[64,384]{1,0:T(8,128)S(1)}, f32[64,384]{1,0:T(8,128)S(1)}, u32[]{:S(2)}, u32[]{:S(2)}) collective-permute-start(f32[64,384]{1,0:T(8,128)S(1)} %fusion.18), channel_id=1, source_target_pairs={{0,28},{4,0},{8,4},{12,8},{16,12},{20,16},{24,20},{28,24},{1,29},{... | collective-permute-start | bytes 294920 | tf_op jit(solution)/shard_map/ppermute | solution.py:17
  232.4 20.6 %collective-permute-start.36 = (f32[64,384]{1,0:T(8,128)S(1)}, f32[64,384]{1,0:T(8,128)S(1)}, u32[]{:S(2)}, u32[]{:S(2)}) collective-permute-start(f32[64,384]{1,0:T(8,128)S(1)} %fusion.6), channel_id=1, source_target_pairs={{0,4},{4,8},{8,12},{12,16},{16,20},{20,24},{24,28},{28,0},{1,5},{5... | collective-permute-start | bytes 294920 | tf_op jit(solution)/shard_map/ppermute | solution.py:17
  242.6 14.6 %collective-permute-start.33 = (f32[64,384]{1,0:T(8,128)S(1)}, f32[64,384]{1,0:T(8,128)S(1)}, u32[]{:S(2)}, u32[]{:S(2)}) collective-permute-start(f32[64,384]{1,0:T(8,128)S(1)} %convolution_add_fusion.8), channel_id=1, source_target_pairs={{0,28},{4,0},{8,4},{12,8},{16,12},{20,16},{24,20},{28,24},{1,29},{... | collective-permute-start | bytes 294920 | tf_op jit(solution)/shard_map/ppermute | solution.py:17
  254.7 6.5 %collective-permute-start.37 = (f32[64,384]{1,0:T(8,128)S(1)}, f32[64,384]{1,0:T(8,128)S(1)}, u32[]{:S(2)}, u32[]{:S(2)}) collective-permute-start(f32[64,384]{1,0:T(8,128)S(1)} %convolution_add_fusion.7), channel_id=1, source_target_pairs={{0,4},{4,8},{8,12},{12,16},{16,20},{20,24},{24,28},{28,0},{1,5},{5... | collective-permute-start | bytes 294920 | tf_op jit(solution)/shard_map/ppermute | solution.py:17
  257.2 7.1 %collective-permute-start.34 = (f32[64,384]{1,0:T(8,128)S(1)}, f32[64,384]{1,0:T(8,128)S(1)}, u32[]{:S(2)}, u32[]{:S(2)}) collective-permute-start(f32[64,384]{1,0:T(8,128)S(1)} %add.427), channel_id=1, source_target_pairs={{0,28},{4,0},{8,4},{12,8},{16,12},{20,16},{24,20},{28,24},{1,29},{... | collective-permute-start | bytes 294920 | tf_op jit(solution)/shard_map/ppermute | solution.py:17
  261.2 6.4 %collective-permute-start.38 = (f32[64,384]{1,0:T(8,128)S(1)}, f32[64,384]{1,0:T(8,128)S(1)}, u32[]{:S(2)}, u32[]{:S(2)}) collective-permute-start(f32[64,384]{1,0:T(8,128)S(1)} %add.431), channel_id=1, source_target_pairs={{0,4},{4,8},{8,12},{12,16},{16,20},{20,24},{24,28},{28,0},{1,5},{5... | collective-permute-start | bytes 294920 | tf_op jit(solution)/shard_map/ppermute | solution.py:17
  264.3 7.6 %collective-permute-start.35 = (f32[64,384]{1,0:T(8,128)S(1)}, f32[64,384]{1,0:T(8,128)S(1)}, u32[]{:S(2)}, u32[]{:S(2)}) collective-permute-start(f32[64,384]{1,0:T(8,128)S(1)} %add.428), channel_id=1, source_target_pairs={{0,28},{4,0},{8,4},{12,8},{16,12},{20,16},{24,20},{28,24},{1,29},{... | collective-permute-start | bytes 294920 | tf_op jit(solution)/shard_map/ppermute | solution.py:17
  (60 other events, 546.5 us)
Sparse Core Ops, SparseCore 0:
  8.9 25.1 all-gather.1
  185.2 32.9 reduce-scatter.6
  253.1 27.1 reduce-scatter.4
where the time goes:
time: 345 us; the launch traced here: 344 us
  waiting for transfers between devices  99 us (29%)
  other arithmetic  73.4 us (21%)
  starting transfers between devices  55.6 us (16%)
  blocking collectives  49 us (14%)
  matrix products  47.9 us (14%)
  between operations  13.8 us (4%)
  local copies, waits for them, and re-layouts  5.73 us (2%)
    ppermute x40, waiting for transfers between devices, shifted(): return lax.ppermute(value, axis, pairs)  73.5 us
    ppermute x40, starting transfers between devices, shifted(): return lax.ppermute(value, axis, pairs)  55.5 us
    reduce_sum x1, other arithmetic, pair_weights(): jnp.sum((lists_here[:, :, None] == positions[None, None, :]).astype(jnp.f...  44.8 us
    psum x1, blocking collectives, local(): gram = lax.psum(partial_gram, ('blk', 'sub'))  43.3 us
    dot_general x9, matrix products, pair_weights(): lax.dot_general(block_feats, moving_feats, (((1,), (1,)), ((), ())), pref...  33.6 us
    unnamed x4, waiting for transfers between devices  18.1 us
    dot_general x9, matrix products, product_work(): col_term = jnp.dot(block_eigen, tile, preferred_element_type=jnp.float32)  8.02 us
    reduce_scatter x1, waiting for transfers between devices, to_owners(): return lax.psum_scatter(terms, 'sub', scatter_dimension=1, tiled=True)  7.33 us
  transfers between devices with their start and end apart: 43, of which 20 were waited for; matrix products, arithmetic and copies ran while one was open for 30% of the time, Pallas kernels for 0%

commit v1 on v0

--- a/solution.py
+++ b/solution.py
@@ -1,3 +1,4 @@
+import functools
 import math
 import jax
 import jax.numpy as jnp
@@ -5,6 +6,14 @@
 from jax.sharding import PartitionSpec as P
 
 F = 768
+
+
+def wall_produce(block_in, chip_axis, axis_tag):
+    s_next = lax.psum(lax.psum(block_in, axis_name=axis_tag), axis_name=chip_axis)
+    return s_next
+
+
+perform_layers_all_up = functools.partial(wall_produce, chip_axis="blk", axis_tag="sub")
 
 
 def as_sent(value):
@@ -105,7 +114,7 @@
     partial_gram = jnp.dot(
         mixed, mixed.T, precision=lax.Precision.HIGHEST, preferred_element_type=jnp.float32
     )
-    gram = lax.psum(partial_gram, ("blk", "sub"))
+    gram = perform_layers_all_up(partial_gram)
     lower = jnp.linalg.cholesky(gram)
     total_rows = rows_dev * lax.axis_size("blk") * lax.axis_size("sub")
     return math.sqrt(total_rows) * jax.scipy.linalg.solve_triangular(lower, mixed, lower=True)

time: 345 us -> 351 us (1.017); the launches traced: 344 us -> 345 us
    psum x1 -> x2, blocking collectives: 43.3 us -> 43.4 us  [the longest x1 33 us: wall_produce(): lax.psum(lax.psum(block_in, axis_name=axis_tag), axis_name=chip_axis)]
where the time goes in v1:
time: 351 us; the launch traced here: 345 us
  waiting for transfers between devices  99 us (28%)
  other arithmetic  73.4 us (21%)
  starting transfers between devices  55.6 us (16%)
  blocking collectives  49.2 us (14%)
  matrix products  47.9 us (14%)
  between operations  13.8 us (4%)
  local copies, waits for them, and re-layouts  5.73 us (2%)
    ppermute x40, waiting for transfers between devices, shifted(): return lax.ppermute(value, axis, pairs)  73.5 us
    ppermute x40, starting transfers between devices, shifted(): return lax.ppermute(value, axis, pairs)  55.5 us
    reduce_sum x1, other arithmetic, pair_weights(): jnp.sum((lists_here[:, :, None] == positions[None, None, :]).astype(jnp.f...  44.8 us
    dot_general x9, matrix products, pair_weights(): lax.dot_general(block_feats, moving_feats, (((1,), (1,)), ((), ())), pref...  33.6 us
    psum x1, blocking collectives, wall_produce(): lax.psum(lax.psum(block_in, axis_name=axis_tag), axis_name=chip_axis)  33 us
    unnamed x4, waiting for transfers between devices  18.1 us
    psum x1, blocking collectives, wall_produce(): lax.psum(block_in, axis_name=axis_tag)  10.4 us
    dot_general x9, matrix products, product_work(): col_term = jnp.dot(block_eigen, tile, preferred_element_type=jnp.float32)  8.02 us
  transfers between devices with their start and end apart: 43, of which 20 were waited for; matrix products, arithmetic and copies ran while one was open for 30% of the time, Pallas kernels for 0%

profile of v1, /device:TPU:10, one launch (start us, length us, event | category | flops | bytes accessed | tf_op | source)
XLA Modules:
  0.0 344.6 jit_solution(16006190981055517272)
XLA Ops:
  15.0 20.4 %collective-permute-done.1 = bf16[384]{0:T(512)(128)(2,1)S(1)} collective-permute-done((bf16[384]{0:T(512)(128)(2,1)S(1)}, bf16[384]{0:T(512)(128)(2,1)S(1)}, u32[]{:S(2)}, u32[]{:S(2)}) %collective-permute-start.1) | collective-permute-done | bytes 800 | tf_op jit(solution)/shard_map/ppermute | solution.py:26
  39.4 44.8 %convert_reduce_fusion.7 = (f32[1536,384]{1,0:T(8,128)}, f32[1536,384]{1,0:T(8,128)}, f32[1536,384]{1,0:T(8,128)}, f32[1536,384]{1,0:T(8,128)}, f32[1536,384]{1,...) fusion(s32[16,1536]{1,0:T(8,128)S(1)} %get-tuple-element.40, ...), kind=kLoop, calls=%fused_computation.7 | loop fusion | flops 249495552 | bytes 22119936 | tf_op jit(solution)/shard_map/reduce_sum | solution.py:39
  84.3 2.4 collective-permute-start.5
  86.7 2.9 collective-permute-start.4
  97.1 15.2 %collective-permute-done.7 = bf16[384]{0:T(512)(128)(2,1)S(1)} collective-permute-done((bf16[384]{0:T(512)(128)(2,1)S(1)}, bf16[384]{0:T(512)(128)(2,1)S(1)}, u32[]{:S(2)}, u32[]{:S(2)}) %collective-permute-start.7) | collective-permute-done | bytes 800 | tf_op jit(solution)/shard_map/ppermute | solution.py:26
  119.7 6.8 %collective-permute-done.6 = bf16[384,768]{1,0:T(8,128)(2,1)S(1)} collective-permute-done((bf16[384,768]{1,0:T(8,128)(2,1)S(1)}, bf16[384,768]{1,0:T(8,128)(2,1)S(1)}, u32[]{:S(2)}, u32[]{:S(2)}) %collective-permute-start.6) | collective-permute-done | bytes 589856 | tf_op jit(solution)/shard_map/ppermute | solution.py:26
  127.3 14.6 %collective-permute-done.14 = bf16[384,768]{1,0:T(8,128)(2,1)S(1)} collective-permute-done((bf16[384,768]{1,0:T(8,128)(2,1)S(1)}, bf16[384,768]{1,0:T(8,128)(2,1)S(1)}, u32[]{:S(2)}, u32[]{:S(2)}) %collective-permute-start.14) | collective-permute-done | bytes 589856 | tf_op jit(solution)/shard_map/ppermute | solution.py:26
  143.5 2.3 multiply_reduce_fusion
  145.9 4.2 %fusion.40 = (f32[384]{0:T(512)S(1)}, f32[1536]{0:T(1024)S(1)}, bf16[1536,384]{1,0:T(8,128)(2,1)S(1)}) fusion(f32[1536,384]{1,0:T(8,128)} %get-tuple-element.26, f32[384]{0:T(512)} %convert_element_type.159, f32[1536]{0:T(1024)S(1)} %convert_multiply_fusion, bf16[1536,768]{1,0:T(8,128)(2,1)S(1)} %copy-done.8, bf16[384,768]{1,0:T(8,128)(2,1)} %copy-done.26, ...), kind=kOutput, calls=%fused_computation.114 | convolution fusion | flops 911865984 | bytes 6511104 | tf_op jit(solution)/shard_map/dot_general | solution.py:32
  152.7 3.4 fusion.44
  157.7 4.0 %fusion.39 = (f32[384]{0:T(512)}, f32[1536]{0:T(1024)S(1)}, bf16[1536,384]{1,0:T(8,128)(2,1)}) fusion(f32[1536,384]{1,0:T(8,128)S(1)} %copy-done.16, f32[384]{0:T(512)S(1)} %copy-done.41, f32[1536]{0:T(1024)S(1)} %convert_multiply_fusion, bf16[1536,768]{1,0:T(8,128)(2,1)S(1)} %copy-done.8, bf16[384,768]{1,0:T(8,128)(2,1)S(1)} %copy-done.23, ...), kind=kOutput, calls=%fused_computation.113 | convolution fusion | flops 911865984 | bytes 6511104 | tf_op jit(solution)/shard_map/dot_general | solution.py:32
  161.7 4.0 %fusion.38 = (f32[384]{0:T(512)}, f32[1536]{0:T(1024)S(1)}, bf16[1536,384]{1,0:T(8,128)(2,1)}) fusion(f32[1536,384]{1,0:T(8,128)S(1)} %copy-done.15, f32[384]{0:T(512)S(1)} %copy-done.40, f32[1536]{0:T(1024)S(1)} %convert_multiply_fusion, bf16[1536,768]{1,0:T(8,128)(2,1)S(1)} %copy-done.8, bf16[384,768]{1,0:T(8,128)(2,1)S(1)} %copy-done.19, ...), kind=kOutput, calls=%fused_computation.112 | convolution fusion | flops 911865984 | bytes 6511104 | tf_op jit(solution)/shard_map/dot_general | solution.py:32
  165.7 3.9 %fusion.37 = (f32[384]{0:T(512)}, f32[1536]{0:T(1024)S(1)}, bf16[1536,384]{1,0:T(8,128)(2,1)}) fusion(f32[1536,384]{1,0:T(8,128)S(1)} %copy-done.14, f32[384]{0:T(512)S(1)} %copy-done.38, f32[1536]{0:T(1024)S(1)} %convert_multiply_fusion, bf16[1536,768]{1,0:T(8,128)(2,1)S(1)} %copy-done.8, bf16[384,768]{1,0:T(8,128)(2,1)S(1)} %collective-permute-done, ...), kind=kOutput, calls=%fused_computation.111 | convolution fusion | flops 911865984 | bytes 6511104 | tf_op jit(solution)/shard_map/dot_general | solution.py:32
  169.7 3.9 %fusion.43 = (f32[384]{0:T(512)}, f32[1536]{0:T(1024)S(1)}, bf16[1536,384]{1,0:T(8,128)(2,1)}) fusion(f32[1536,384]{1,0:T(8,128)S(1)} %copy-done.13, f32[384]{0:T(512)S(1)} %copy-done.39, f32[1536]{0:T(1024)S(1)} %convert_multiply_fusion, bf16[1536,768]{1,0:T(8,128)(2,1)S(1)} %copy-done.8, bf16[384,768]{1,0:T(8,128)(2,1)S(1)} %copy-done.21, ...), kind=kOutput, calls=%fused_computation.117 | convolution fusion | flops 911865984 | bytes 6511104 | tf_op jit(solution)/shard_map/dot_general | solution.py:32
  173.7 4.1 %fusion.42 = (f32[384]{0:T(512)}, f32[1536]{0:T(1024)S(1)}, bf16[1536,384]{1,0:T(8,128)(2,1)}) fusion(f32[1536,384]{1,0:T(8,128)S(1)} %copy-done.12, f32[384]{0:T(512)S(1)} %copy-done.37, f32[1536]{0:T(1024)S(1)} %convert_multiply_fusion, bf16[1536,768]{1,0:T(8,128)(2,1)S(1)} %copy-done.8, bf16[384,768]{1,0:T(8,128)(2,1)S(1)} %collective-permute-done.10, ...), kind=kOutput, calls=%fused_computation.116 | convolution fusion | flops 911865984 | bytes 6511104 | tf_op jit(solution)/shard_map/dot_general | solution.py:32
  177.7 3.4 fusion.41
  181.2 2.6 fusion.36
  185.8 5.4 %collective-permute-start.17 = (f32[1,384]{1,0:T(1,128)S(1)}, f32[1,384]{1,0:T(1,128)S(1)}, u32[]{:S(2)}, u32[]{:S(2)}) collective-permute-start(f32[1,384]{1,0:T(1,128)S(1)} %reshape_add_fusion.5), channel_id=1, source_target_pairs={{0,28},{4,0},{8,4},{12,8},{16,12},{20,16},{24,20},{28,24},{1,29},{... | collective-permute-start | bytes 4616 | tf_op jit(solution)/shard_map/ppermute | solution.py:26
  192.5 2.9 collective-permute-start.18
  197.0 2.9 collective-permute-start.19
  200.9 17.3 %reduce-scatter.7.cloned.1.call-done = f32[384,1]{1,0:T(8,128)} async-done(((f32[1536,1]{1,0:T(8,128)}), f32[384,1]{1,0:T(8,128)}) %reduce-scatter.7.cloned.1.call-update) | async-done | bytes 1552
  219.3 5.7 %all_gather.7 = bf16[64,1536]{1,0:T(8,128)(2,1)S(1)} all-gather(bf16[64,384]{1,0:T(8,128)(2,1)S(1)} %multiply_convert_fusion), channel_id=1, replica_groups=mesh['blk'=8,'sub'=4] {'sub'}, dimensions={1}, use_global_device_ids=true | all-gather | bytes 245760 | tf_op jit(solution)/shard_map/all_gather | solution.py:100
  237.6 2.1 collective-permute-done.25
  257.2 2.6 collective-permute-start.34
  261.6 2.7 collective-permute-done.34
  264.3 2.5 collective-permute-start.35
  269.7 2.2 collective-permute-done.35
  273.0 7.3 %reduce-scatter.5.cloned.1.call-done = f32[64,384]{1,0:T(8,128)} async-done(((f32[64,1536]{1,0:T(8,128)}), f32[64,384]{1,0:T(8,128)}) %reduce-scatter.5.cloned.1.call-update) | async-done | bytes 98320 | tf_op jit(solution)/shard_map/reduce_scatter | solution.py:67
  281.5 10.4 %psum.14 = f32[64,64]{0,1:T(8,128)S(1)} all-reduce(f32[64,64]{0,1:T(8,128)S(1)} %fusion.46), channel_id=1, replica_groups=mesh['blk'=8,'sub'=4] {'sub'}, use_global_device_ids=true, to_apply=%region_39.0 | all-reduce | flops 4096 | bytes 32768 | tf_op jit(solution)/shard_map/psum | solution.py:12
  291.9 33.0 %psum.15 = f32[64,64]{0,1:T(8,128)S(1)} all-reduce(f32[64,64]{0,1:T(8,128)S(1)} %psum.14), channel_id=1, replica_groups=mesh['blk'=8,'sub'=4] {'blk'}, use_global_device_ids=true, to_apply=%region_40.0 | all-reduce | flops 4096 | bytes 32768 | tf_op jit(solution)/shard_map/psum | solution.py:12
  325.0 5.8 %cholesky.16 = f32[64,64]{1,0:T(8,128)S(1)} custom-call(f32[64,64]{1,0:T(8,128)S(1)} %fusion.35), custom_call_target="Cholesky" | custom-call | tf_op jit(solution)/shard_map/jit(cholesky)/cholesky | solution.py:118
  332.2 4.9 %custom-call.7 = f32[1,64,64]{1,2,0:T(8,128)S(1)} custom-call(f32[1,64,64]{2,1,0:T(8,128)S(1)} %fusion.33), custom_call_target="InvertDiagBlocksLowerTriangular" | custom-call | tf_op jit(solution)/shard_map/jit(_solve_triangular)/triangular_solve | solution.py:120
  (235 shorter events, 79.7 us)
Async XLA Ops:
  6.5 136.9 %all-gather.2.cloned.1.call-start = ((), (), s32[]{:S(2)}) async-start(), calls=%async_computation.2 | async-start | bytes 2949120 | tf_op jit(solution)/shard_map/all_gather | solution.py:74
  7.3 210.9 %reduce-scatter.7.cloned.1.call-start = ((), (), s32[]{:S(2)}) async-start(), calls=%async_computation.4 | async-start | bytes 983040
  7.3 30.1 %collective-permute-start = (bf16[384,768]{1,0:T(8,128)(2,1)}, bf16[384,768]{1,0:T(8,128)(2,1)S(1)}, u32[]{:S(2)}, u32[]{:S(2)}) collective-permute-start(bf16[384,768]{1,0:T(8,128)(2,1)} %param.4), channel_id=1, source_target_pairs={{0,4},{4,8},{8,12},{12,16},{16,20},{20,24},{24,28},{28,0},{1,5},{5... | collective-permute-start | bytes 1769480 | tf_op jit(solution)/shard_map/ppermute | solution.py:26
  10.2 25.1 %collective-permute-start.1 = (bf16[384]{0:T(512)(128)(2,1)S(1)}, bf16[384]{0:T(512)(128)(2,1)S(1)}, u32[]{:S(2)}, u32[]{:S(2)}) collective-permute-start(bf16[384]{0:T(512)(128)(2,1)S(1)} %get-tuple-element.33), channel_id=1, source_target_pairs={{0,4},{4,8},{8,12},{12,16},{16,20},{20,24},{24,28},{28,0},{1,5},{5... | collective-permute-start | bytes 2312 | tf_op jit(solution)/shard_map/ppermute | solution.py:26
  11.7 24.2 %collective-permute-start.9 = (bf16[384]{0:T(512)(128)(2,1)S(1)}, bf16[384]{0:T(512)(128)(2,1)S(1)}, u32[]{:S(2)}, u32[]{:S(2)}) collective-permute-start(bf16[384]{0:T(512)(128)(2,1)S(1)} %get-tuple-element.33), channel_id=1, source_target_pairs={{0,28},{4,0},{8,4},{12,8},{16,12},{20,16},{24,20},{28,24},{1,29},{... | collective-permute-start | bytes 2312 | tf_op jit(solution)/shard_map/ppermute | solution.py:26
  12.3 26.6 %collective-permute-start.8 = (bf16[384,768]{1,0:T(8,128)(2,1)}, bf16[384,768]{1,0:T(8,128)(2,1)S(1)}, u32[]{:S(2)}, u32[]{:S(2)}) collective-permute-start(bf16[384,768]{1,0:T(8,128)(2,1)} %param.4), channel_id=1, source_target_pairs={{0,28},{4,0},{8,4},{12,8},{16,12},{20,16},{24,20},{28,24},{1,29},{... | collective-permute-start | bytes 1769480 | tf_op jit(solution)/shard_map/ppermute | solution.py:26
  35.4 48.9 %collective-permute-start.3 = (bf16[384]{0:T(512)(128)(2,1)S(1)}, bf16[384]{0:T(512)(128)(2,1)S(1)}, u32[]{:S(2)}, u32[]{:S(2)}) collective-permute-start(bf16[384]{0:T(512)(128)(2,1)S(1)} %collective-permute-done.1), channel_id=1, source_target_pairs={{0,4},{4,8},{8,12},{12,16},{16,20},{20,24},{24,28},{28,0},{1,5},{5... | collective-permute-start | bytes 2312 | tf_op jit(solution)/shard_map/ppermute | solution.py:26
  36.0 50.7 %collective-permute-start.11 = (bf16[384]{0:T(512)(128)(2,1)S(1)}, bf16[384]{0:T(512)(128)(2,1)S(1)}, u32[]{:S(2)}, u32[]{:S(2)}) collective-permute-start(bf16[384]{0:T(512)(128)(2,1)S(1)} %collective-permute-done.9), channel_id=1, source_target_pairs={{0,28},{4,0},{8,4},{12,8},{16,12},{20,16},{24,20},{28,24},{1,29},{... | collective-permute-start | bytes 2312 | tf_op jit(solution)/shard_map/ppermute | solution.py:26
  37.4 49.3 %collective-permute-start.2 = (bf16[384,768]{1,0:T(8,128)(2,1)S(1)}, bf16[384,768]{1,0:T(8,128)(2,1)S(1)}, u32[]{:S(2)}, u32[]{:S(2)}) collective-permute-start(bf16[384,768]{1,0:T(8,128)(2,1)S(1)} %collective-permute-done), channel_id=1, source_target_pairs={{0,4},{4,8},{8,12},{12,16},{16,20},{20,24},{24,28},{28,0},{1,5},{5... | collective-permute-start | bytes 1769480 | tf_op jit(solution)/shard_map/ppermute | solution.py:26
  38.9 52.8 %collective-permute-start.10 = (bf16[384,768]{1,0:T(8,128)(2,1)S(1)}, bf16[384,768]{1,0:T(8,128)(2,1)S(1)}, u32[]{:S(2)}, u32[]{:S(2)}) collective-permute-start(bf16[384,768]{1,0:T(8,128)(2,1)S(1)} %collective-permute-done.8), channel_id=1, source_target_pairs={{0,28},{4,0},{8,4},{12,8},{16,12},{20,16},{24,20},{28,24},{1,29},{... | collective-permute-start | bytes 1769480 | tf_op jit(solution)/shard_map/ppermute | solution.py:26
  84.3 5.4 %collective-permute-start.5 = (bf16[384]{0:T(512)(128)(2,1)S(1)}, bf16[384]{0:T(512)(128)(2,1)S(1)}, u32[]{:S(2)}, u32[]{:S(2)}) collective-permute-start(bf16[384]{0:T(512)(128)(2,1)S(1)} %collective-permute-done.3), channel_id=1, source_target_pairs={{0,4},{4,8},{8,12},{12,16},{16,20},{20,24},{24,28},{28,0},{1,5},{5... | collective-permute-start | bytes 2312 | tf_op jit(solution)/shard_map/ppermute | solution.py:26
  86.7 27.8 %collective-permute-start.4 = (bf16[384,768]{1,0:T(8,128)(2,1)S(1)}, bf16[384,768]{1,0:T(8,128)(2,1)S(1)}, u32[]{:S(2)}, u32[]{:S(2)}) collective-permute-start(bf16[384,768]{1,0:T(8,128)(2,1)S(1)} %collective-permute-done.2), channel_id=1, source_target_pairs={{0,4},{4,8},{8,12},{12,16},{16,20},{20,24},{24,28},{28,0},{1,5},{5... | collective-permute-start | bytes 1769480 | tf_op jit(solution)/shard_map/ppermute | solution.py:26
  89.6 22.7 %collective-permute-start.7 = (bf16[384]{0:T(512)(128)(2,1)S(1)}, bf16[384]{0:T(512)(128)(2,1)S(1)}, u32[]{:S(2)}, u32[]{:S(2)}) collective-permute-start(bf16[384]{0:T(512)(128)(2,1)S(1)} %collective-permute-done.5), channel_id=1, source_target_pairs={{0,4},{4,8},{8,12},{12,16},{16,20},{20,24},{24,28},{28,0},{1,5},{5... | collective-permute-start | bytes 2312 | tf_op jit(solution)/shard_map/ppermute | solution.py:26
  91.2 21.7 %collective-permute-start.15 = (bf16[384]{0:T(512)(128)(2,1)S(1)}, bf16[384]{0:T(512)(128)(2,1)S(1)}, u32[]{:S(2)}, u32[]{:S(2)}) collective-permute-start(bf16[384]{0:T(512)(128)(2,1)S(1)} %collective-permute-done.13), channel_id=1, source_target_pairs={{0,28},{4,0},{8,4},{12,8},{16,12},{20,16},{24,20},{28,24},{1,29},{... | collective-permute-start | bytes 2312 | tf_op jit(solution)/shard_map/ppermute | solution.py:26
  91.7 24.2 %collective-permute-start.12 = (bf16[384,768]{1,0:T(8,128)(2,1)S(1)}, bf16[384,768]{1,0:T(8,128)(2,1)S(1)}, u32[]{:S(2)}, u32[]{:S(2)}) collective-permute-start(bf16[384,768]{1,0:T(8,128)(2,1)S(1)} %collective-permute-done.10), channel_id=1, source_target_pairs={{0,28},{4,0},{8,4},{12,8},{16,12},{20,16},{24,20},{28,24},{1,29},{... | collective-permute-start | bytes 1769480 | tf_op jit(solution)/shard_map/ppermute | solution.py:26
  114.5 12.0 %collective-permute-start.6 = (bf16[384,768]{1,0:T(8,128)(2,1)S(1)}, bf16[384,768]{1,0:T(8,128)(2,1)S(1)}, u32[]{:S(2)}, u32[]{:S(2)}) collective-permute-start(bf16[384,768]{1,0:T(8,128)(2,1)S(1)} %collective-permute-done.4), channel_id=1, source_target_pairs={{0,4},{4,8},{8,12},{12,16},{16,20},{20,24},{24,28},{28,0},{1,5},{5... | collective-permute-start | bytes 1769480 | tf_op jit(solution)/shard_map/ppermute | solution.py:26
  115.9 26.0 %collective-permute-start.14 = (bf16[384,768]{1,0:T(8,128)(2,1)S(1)}, bf16[384,768]{1,0:T(8,128)(2,1)S(1)}, u32[]{:S(2)}, u32[]{:S(2)}) collective-permute-start(bf16[384,768]{1,0:T(8,128)(2,1)S(1)} %collective-permute-done.12), channel_id=1, source_target_pairs={{0,28},{4,0},{8,4},{12,8},{16,12},{20,16},{24,20},{28,24},{1,29},{... | collective-permute-start | bytes 1769480 | tf_op jit(solution)/shard_map/ppermute | solution.py:26
  150.7 34.4 %collective-permute-start.16 = (f32[1,384]{1,0:T(1,128)}, f32[1,384]{1,0:T(1,128)}, u32[]{:S(2)}, u32[]{:S(2)}) collective-permute-start(f32[1,384]{1,0:T(1,128)} %broadcast_in_dim.20), channel_id=1, source_target_pairs={{0,28},{4,0},{8,4},{12,8},{16,12},{20,16},{24,20},{28,24},{1,29},{... | collective-permute-start | bytes 4616 | tf_op jit(solution)/shard_map/ppermute | solution.py:26
  156.7 34.5 %collective-permute-start.20 = (f32[1,384]{1,0:T(1,128)}, f32[1,384]{1,0:T(1,128)}, u32[]{:S(2)}, u32[]{:S(2)}) collective-permute-start(f32[1,384]{1,0:T(1,128)} %broadcast_in_dim.24), channel_id=1, source_target_pairs={{0,4},{4,8},{8,12},{12,16},{16,20},{20,24},{24,28},{28,0},{1,5},{5... | collective-permute-start | bytes 4616 | tf_op jit(solution)/shard_map/ppermute | solution.py:26
  185.1 95.2 %reduce-scatter.5.cloned.1.call-start = ((), (), s32[]{:S(2)}) async-start(), calls=%async_computation.3 | async-start | bytes 491520 | tf_op jit(solution)/shard_map/reduce_scatter | solution.py:67
  185.8 6.7 %collective-permute-start.17 = (f32[1,384]{1,0:T(1,128)S(1)}, f32[1,384]{1,0:T(1,128)S(1)}, u32[]{:S(2)}, u32[]{:S(2)}) collective-permute-start(f32[1,384]{1,0:T(1,128)S(1)} %reshape_add_fusion.5), channel_id=1, source_target_pairs={{0,28},{4,0},{8,4},{12,8},{16,12},{20,16},{24,20},{28,24},{1,29},{... | collective-permute-start | bytes 4616 | tf_op jit(solution)/shard_map/ppermute | solution.py:26
  197.0 22.2 %collective-permute-start.19 = (f32[1,384]{1,0:T(1,128)S(1)}, f32[1,384]{1,0:T(1,128)S(1)}, u32[]{:S(2)}, u32[]{:S(2)}) collective-permute-start(f32[1,384]{1,0:T(1,128)S(1)} %reshape_add_fusion.3), channel_id=1, source_target_pairs={{0,28},{4,0},{8,4},{12,8},{16,12},{20,16},{24,20},{28,24},{1,29},{... | collective-permute-start | bytes 4616 | tf_op jit(solution)/shard_map/ppermute | solution.py:26
  200.9 18.4 %collective-permute-start.23 = (f32[1,384]{1,0:T(1,128)S(1)}, f32[1,384]{1,0:T(1,128)S(1)}, u32[]{:S(2)}, u32[]{:S(2)}) collective-permute-start(f32[1,384]{1,0:T(1,128)S(1)} %reshape_add_fusion), channel_id=1, source_target_pairs={{0,4},{4,8},{8,12},{12,16},{16,20},{20,24},{24,28},{28,0},{1,5},{5... | collective-permute-start | bytes 4616 | tf_op jit(solution)/shard_map/ppermute | solution.py:26
  225.0 9.4 %collective-permute-start.24 = (bf16[64,384]{1,0:T(8,128)(2,1)S(1)}, bf16[64,384]{1,0:T(8,128)(2,1)S(1)}, u32[]{:S(2)}, u32[]{:S(2)}) collective-permute-start(bf16[64,384]{1,0:T(8,128)(2,1)S(1)} %multiply_convert_fusion), channel_id=1, source_target_pairs={{0,4},{4,8},{8,12},{12,16},{16,20},{20,24},{24,28},{28,0},{1,5},{5... | collective-permute-start | bytes 147464 | tf_op jit(solution)/shard_map/ppermute | solution.py:26
  226.5 10.0 %collective-permute-start.28 = (bf16[64,384]{1,0:T(8,128)(2,1)S(1)}, bf16[64,384]{1,0:T(8,128)(2,1)S(1)}, u32[]{:S(2)}, u32[]{:S(2)}) collective-permute-start(bf16[64,384]{1,0:T(8,128)(2,1)S(1)} %multiply_convert_fusion), channel_id=1, source_target_pairs={{0,28},{4,0},{8,4},{12,8},{16,12},{20,16},{24,20},{28,24},{1,29},{... | collective-permute-start | bytes 147464 | tf_op jit(solution)/shard_map/ppermute | solution.py:26
  230.6 11.7 %collective-permute-start.32 = (f32[64,384]{1,0:T(8,128)S(1)}, f32[64,384]{1,0:T(8,128)S(1)}, u32[]{:S(2)}, u32[]{:S(2)}) collective-permute-start(f32[64,384]{1,0:T(8,128)S(1)} %fusion.18), channel_id=1, source_target_pairs={{0,28},{4,0},{8,4},{12,8},{16,12},{20,16},{24,20},{28,24},{1,29},{... | collective-permute-start | bytes 294920 | tf_op jit(solution)/shard_map/ppermute | solution.py:26
  232.4 20.6 %collective-permute-start.36 = (f32[64,384]{1,0:T(8,128)S(1)}, f32[64,384]{1,0:T(8,128)S(1)}, u32[]{:S(2)}, u32[]{:S(2)}) collective-permute-start(f32[64,384]{1,0:T(8,128)S(1)} %fusion.6), channel_id=1, source_target_pairs={{0,4},{4,8},{8,12},{12,16},{16,20},{20,24},{24,28},{28,0},{1,5},{5... | collective-permute-start | bytes 294920 | tf_op jit(solution)/shard_map/ppermute | solution.py:26
  242.6 14.6 %collective-permute-start.33 = (f32[64,384]{1,0:T(8,128)S(1)}, f32[64,384]{1,0:T(8,128)S(1)}, u32[]{:S(2)}, u32[]{:S(2)}) collective-permute-start(f32[64,384]{1,0:T(8,128)S(1)} %convolution_add_fusion.8), channel_id=1, source_target_pairs={{0,28},{4,0},{8,4},{12,8},{16,12},{20,16},{24,20},{28,24},{1,29},{... | collective-permute-start | bytes 294920 | tf_op jit(solution)/shard_map/ppermute | solution.py:26
  254.7 6.5 %collective-permute-start.37 = (f32[64,384]{1,0:T(8,128)S(1)}, f32[64,384]{1,0:T(8,128)S(1)}, u32[]{:S(2)}, u32[]{:S(2)}) collective-permute-start(f32[64,384]{1,0:T(8,128)S(1)} %convolution_add_fusion.7), channel_id=1, source_target_pairs={{0,4},{4,8},{8,12},{12,16},{16,20},{20,24},{24,28},{28,0},{1,5},{5... | collective-permute-start | bytes 294920 | tf_op jit(solution)/shard_map/ppermute | solution.py:26
  257.2 7.1 %collective-permute-start.34 = (f32[64,384]{1,0:T(8,128)S(1)}, f32[64,384]{1,0:T(8,128)S(1)}, u32[]{:S(2)}, u32[]{:S(2)}) collective-permute-start(f32[64,384]{1,0:T(8,128)S(1)} %add.429), channel_id=1, source_target_pairs={{0,28},{4,0},{8,4},{12,8},{16,12},{20,16},{24,20},{28,24},{1,29},{... | collective-permute-start | bytes 294920 | tf_op jit(solution)/shard_map/ppermute | solution.py:26
  261.2 6.4 %collective-permute-start.38 = (f32[64,384]{1,0:T(8,128)S(1)}, f32[64,384]{1,0:T(8,128)S(1)}, u32[]{:S(2)}, u32[]{:S(2)}) collective-permute-start(f32[64,384]{1,0:T(8,128)S(1)} %add.433), channel_id=1, source_target_pairs={{0,4},{4,8},{8,12},{12,16},{16,20},{20,24},{24,28},{28,0},{1,5},{5... | collective-permute-start | bytes 294920 | tf_op jit(solution)/shard_map/ppermute | solution.py:26
  264.3 7.6 %collective-permute-start.35 = (f32[64,384]{1,0:T(8,128)S(1)}, f32[64,384]{1,0:T(8,128)S(1)}, u32[]{:S(2)}, u32[]{:S(2)}) collective-permute-start(f32[64,384]{1,0:T(8,128)S(1)} %add.430), channel_id=1, source_target_pairs={{0,28},{4,0},{8,4},{12,8},{16,12},{20,16},{24,20},{28,24},{1,29},{... | collective-permute-start | bytes 294920 | tf_op jit(solution)/shard_map/ppermute | solution.py:26
  (60 other events, 546.5 us)
Sparse Core Ops, SparseCore 0:
  8.9 25.1 all-gather.1
  185.2 32.9 reduce-scatter.6
  253.1 27.1 reduce-scatter.4
